TPU v7x, 32 devices: a whole 2x2x4 slice. The times are simulated.
32 devices in a mesh: row: 4 (over x, core), col: 8 (over z, y).
Axes of the slice: x: 2, y: 2, z: 4, core: 2. Of those that a mesh axis runs over, the one named last changes fastest.
Arguments:
- eigvecs: float32 [1024, 1024], P('row', 'col'), may hold values from -6 to 6
- offsets: int32 [1], replicated, may hold values from 0 to 127
- plan: int32 [1, 6], replicated, may hold values from 0 to 7
- refl_v: float32 [8, 255, 128], P('col')
- refl_t: float32 [8, 128, 128], P('col'), as said below
Outputs:
- updated: float32 [1024, 1024], P('row', 'col')
Inputs may be any that keep to these rules, and one draw needn't show every extreme that they name: For each bank entry, I - refl_v refl_t refl_v^T is orthogonal up to rounding.
All inputs are finite; a program needn't handle non-finite values.
Results may differ from a plain program's by a relative error of at most 0.00015.
Values sent between devices are 32-bit elements; how exact they have to be, the bound alone decides.
No kernel may reach another device: no remote copies, remote signals or barrier semaphores. Data moves between devices by JAX's collectives and lax.ppermute only.
A program may use at most 64 MiB of HBM per device.

v0:
```python
import jax
import jax.numpy as jnp
from jax import lax
from jax.sharding import PartitionSpec as P

HIGHEST = lax.Precision.HIGHEST


def apply_one(extended, row_start, vectors, factor, weight):
    span_rows = vectors.shape[0]
    block_rows = lax.dynamic_slice_in_dim(extended, row_start, span_rows, 0)
    inner_prod = jnp.dot(vectors.T, block_rows, precision=HIGHEST)
    scaled = jnp.dot(factor, inner_prod, precision=HIGHEST)
    block_rows = block_rows - weight * jnp.dot(vectors, scaled, precision=HIGHEST)
    return lax.dynamic_update_slice_in_dim(extended, block_rows, row_start, 0)


def on_device(eigvecs, offsets, plan, refl_v, refl_t):
    rows_dev = eigvecs.shape[0]
    band = refl_v.shape[2]
    per_device = rows_dev // band
    row_count = lax.axis_size("row")
    block_total = row_count * per_device - 2
    bank_v, bank_t = (
        lax.all_gather(refl_v, "col", axis=0, tiled=True),
        lax.all_gather(refl_t, "col", axis=0, tiled=True),
    )
    columns = lax.all_to_all(eigvecs, "row", split_axis=1, concat_axis=0, tiled=True)
    first_row = offsets[0]

    def apply_all(index, matrix):
        block_id = plan[0, index]
        row_start = first_row + index * band
        return apply_one(matrix, row_start, bank_v[block_id], bank_t[block_id], 1.0)

    columns = lax.fori_loop(0, block_total, apply_all, columns)
    return lax.all_to_all(columns, "row", split_axis=0, concat_axis=1, tiled=True)


def solution(mesh):
    in_specs = (P("row", "col"), P(), P(), P("col", None, None), P("col", None, None))
    out_specs = P("row", "col")
    return jax.shard_map(
        on_device, mesh=mesh, in_specs=in_specs, out_specs=out_specs, check_vma=False
    )
```

profile of v0, /device:TPU:0, one launch (start us, length us, event | category | flops | bytes accessed | tf_op | source)
XLA Modules:
  0.0 107.6 jit_solution(541290155468602737)
XLA Ops:
  0.0 1.7 %copy.17 = f32[256,128]{0,1:T(8,128)} copy(f32[256,128]{1,0:T(8,128)} %param.7) | data formatting | bytes 262144 | tf_op args[0]
  1.7 4.4 %all-to-all-start = ((f32[256,4,32]{0,2,1:T(8,128)}), f32[256,4,32]{0,2,1:T(8,128)S(1)}, u32[]{:S(2)}, u32[]{:S(2)}) async-start(f32[256,4,32]{0,2,1:T(8,128)} %bitcast.3), calls=%async_computation | async-start | bytes 262144 | tf_op jit(solution)/shard_map/all_to_all | solution.py:28
  6.1 34.2 %all_gather.6 = f32[8,255,128]{2,1,0:T(8,128)S(1)} all-gather(f32[1,255,128]{2,1,0:T(8,128)S(1)} %copy.19), channel_id=1, replica_groups=mesh['row'=4,'col'=8] {'col'}, dimensions={0}, use_global_device_ids=true | all-gather | bytes 1175040 | tf_op jit(solution)/shard_map/all_gather | solution.py:25
  40.3 31.3 %all_gather.7 = f32[8,128,128]{2,1,0:T(8,128)S(1)} all-gather(f32[1,128,128]{2,1,0:T(8,128)S(1)} %copy-done.1), channel_id=1, replica_groups=mesh['row'=4,'col'=8] {'col'}, dimensions={0}, use_global_device_ids=true | all-gather | bytes 589824 | tf_op jit(solution)/shard_map/all_gather | solution.py:26
  71.6 0.6 copy-done.2
  72.3 27.2 %while.13 = (s32[]{:T(128)}, f32[1024,32]{0,1:T(8,128)S(1)}, s32[]{:T(128)}, s32[1,6]{1,0:T(1,128)S(1)}, f32[8,255,128]{2,1,0:T(8,128)S(1)}, /*index=5*/f32[8,12...) while((s32[]{:T(128)}, f32[1024,32]{0,1:T(8,128)S(1)}, ...), condition=%wide.region_1.0_spmd, body=%wide.region_0.0_spmd.sunk | while | flops 31367144 | bytes 556917 | solution.py:36
  72.9 0.6 constant_dynamic-slice_fusion.2
  75.9 0.3 convolution_subtract_fusion.2
  76.2 0.6 dynamic_update_slice.8
  77.5 0.6 constant_dynamic-slice_fusion.2
  80.5 0.3 convolution_subtract_fusion.2
  80.7 0.6 dynamic_update_slice.8
  82.0 0.6 constant_dynamic-slice_fusion.2
  85.0 0.3 convolution_subtract_fusion.2
  85.3 0.6 dynamic_update_slice.8
  86.5 0.6 constant_dynamic-slice_fusion.2
  89.8 0.6 dynamic_update_slice.8
  91.1 0.6 constant_dynamic-slice_fusion.2
  94.3 0.6 dynamic_update_slice.8
  95.6 0.6 constant_dynamic-slice_fusion.2
  98.6 0.3 convolution_subtract_fusion.2
  98.9 0.5 dynamic_update_slice.8
  99.5 7.4 %all_to_all.38 = f32[4,256,32]{1,2,0:T(8,128)S(1)} all-to-all(f32[4,256,32]{1,2,0:T(8,128)S(1)} %bitcast.38), channel_id=1, replica_groups=mesh['row'=4,'col'=8] {'row'}, dimensions={0} | all-to-all | bytes 262144 | tf_op jit(solution)/shard_map/all_to_all | solution.py:37
  106.8 0.8 copy.21
  (23 shorter events, 3.2 us)
Async XLA Ops:
  1.7 4.4 %copy-start = (f32[1,255,128]{2,0,1:T(1,128)S(1)}, f32[1,255,128]{2,0,1:T(1,128)}, u32[]{:S(2)}) copy-start(f32[1,255,128]{2,0,1:T(1,128)} %param.10) | copy-start | bytes 391684
  1.7 69.9 %all-to-all-start = ((f32[256,4,32]{0,2,1:T(8,128)}), f32[256,4,32]{0,2,1:T(8,128)S(1)}, u32[]{:S(2)}, u32[]{:S(2)}) async-start(f32[256,4,32]{0,2,1:T(8,128)} %bitcast.3), calls=%async_computation | async-start | bytes 262144 | tf_op jit(solution)/shard_map/all_to_all | solution.py:28
  6.0 34.2 %copy-start.1 = (f32[1,128,128]{2,1,0:T(8,128)S(1)}, f32[1,128,128]{2,1,0:T(8,128)}, u32[]{:S(2)}) copy-start(f32[1,128,128]{2,1,0:T(8,128)} %param.11) | copy-start | bytes 196612
  71.6 0.7 copy-start.2
where the time goes:
time: 108 us
  blocking collectives  72.9 us (68%)
  loops' own time  15.8 us (15%)
  local copies, waits for them, and re-layouts  10.1 us (9%)
  starting transfers between devices  4.37 us (4%)
  matrix products  4.28 us (4%)
    all_gather x1, blocking collectives, on_device(): lax.all_gather(refl_v, 'col', axis=0, tiled=True)  34.2 us
    all_gather x1, blocking collectives, on_device(): lax.all_gather(refl_t, 'col', axis=0, tiled=True)  31.3 us
    another operation x1, loops' own time, on_device(): columns = lax.fori_loop(0, block_total, apply_all, columns)  15.8 us
    all_to_all x1, blocking collectives, on_device(): lax.all_to_all(columns, 'row', split_axis=0, concat_axis=1, tiled=True)  7.4 us
    all_to_all x1, starting transfers between devices, on_device(): lax.all_to_all(eigvecs, 'row', split_axis=1, concat_axis=0, tiled=True)  4.37 us
    dynamic_update_slice x6, local copies, waits for them, and re-layouts, apply_one(): return lax.dynamic_update_slice_in_dim(extended, block_rows, row_start, 0)  3.52 us
    dynamic_slice x6, local copies, waits for them, and re-layouts, apply_all(): block_id = plan[0, index]  3.51 us
    unnamed x8, local copies, waits for them, and re-layouts  2.33 us
  transfers between devices with their start and end apart: 1, of which 0 were waited for; matrix products, arithmetic and copies ran while one was open for 0% of the time, Pallas kernels for 0%

commit v1 on v0

--- a/solution.py
+++ b/solution.py
@@ -4,6 +4,13 @@
 from jax.sharding import PartitionSpec as P
 
 HIGHEST = lax.Precision.HIGHEST
+
+
+def exchange_blocks(x, mesh_axis, split, join):
+    devices = lax.axis_size(mesh_axis)
+    blocks = jnp.stack(jnp.split(x, devices, axis=split), axis=0)
+    blocks = lax.all_to_all(blocks, mesh_axis, split_axis=0, concat_axis=0)
+    return jnp.concatenate(blocks, axis=join)
 
 
 def apply_one(extended, row_start, vectors, factor, weight):
@@ -34,7 +41,7 @@
         return apply_one(matrix, row_start, bank_v[block_id], bank_t[block_id], 1.0)
 
     columns = lax.fori_loop(0, block_total, apply_all, columns)
-    return lax.all_to_all(columns, "row", split_axis=0, concat_axis=1, tiled=True)
+    return exchange_blocks(columns, "row", 0, 1)
 
 
 def solution(mesh):

time: 108 us -> 108 us (level)
  no operation moved by 1% of the time
where the time goes in v1:
time: 108 us
  blocking collectives  72.9 us (68%)
  loops' own time  15.8 us (15%)
  local copies, waits for them, and re-layouts  10.1 us (9%)
  starting transfers between devices  4.37 us (4%)
  matrix products  4.28 us (4%)
    all_gather x1, blocking collectives, on_device(): lax.all_gather(refl_v, 'col', axis=0, tiled=True)  34.2 us
    all_gather x1, blocking collectives, on_device(): lax.all_gather(refl_t, 'col', axis=0, tiled=True)  31.3 us
    another operation x1, loops' own time, on_device(): columns = lax.fori_loop(0, block_total, apply_all, columns)  15.8 us
    all_to_all x1, blocking collectives, exchange_blocks(): blocks = lax.all_to_all(blocks, mesh_axis, split_axis=0, concat_axis=0)  7.4 us
    all_to_all x1, starting transfers between devices, on_device(): lax.all_to_all(eigvecs, 'row', split_axis=1, concat_axis=0, tiled=True)  4.37 us
    dynamic_update_slice x6, local copies, waits for them, and re-layouts, apply_one(): return lax.dynamic_update_slice_in_dim(extended, block_rows, row_start, 0)  3.52 us
    dynamic_slice x6, local copies, waits for them, and re-layouts, apply_all(): block_id = plan[0, index]  3.51 us
    unnamed x8, local copies, waits for them, and re-layouts  2.33 us
  transfers between devices with their start and end apart: 1, of which 0 were waited for; matrix products, arithmetic and copies ran while one was open for 0% of the time, Pallas kernels for 0%

profile of v1, /device:TPU:0, one launch (start us, length us, event | category | flops | bytes accessed | tf_op | source)
XLA Modules:
  0.0 107.6 jit_solution(8041815645970762)
XLA Ops:
  0.0 1.7 %copy.16 = f32[256,128]{0,1:T(8,128)} copy(f32[256,128]{1,0:T(8,128)} %param.7) | data formatting | bytes 262144 | tf_op args[0]
  1.7 4.4 %all-to-all-start = ((f32[256,4,32]{0,2,1:T(8,128)}), f32[256,4,32]{0,2,1:T(8,128)S(1)}, u32[]{:S(2)}, u32[]{:S(2)}) async-start(f32[256,4,32]{0,2,1:T(8,128)} %bitcast.3), calls=%async_computation | async-start | bytes 262144 | tf_op jit(solution)/shard_map/all_to_all | solution.py:35
  6.1 34.2 %all_gather.6 = f32[8,255,128]{2,1,0:T(8,128)S(1)} all-gather(f32[1,255,128]{2,1,0:T(8,128)S(1)} %copy.18), channel_id=1, replica_groups=mesh['row'=4,'col'=8] {'col'}, dimensions={0}, use_global_device_ids=true | all-gather | bytes 1175040 | tf_op jit(solution)/shard_map/all_gather | solution.py:32
  40.3 31.3 %all_gather.7 = f32[8,128,128]{2,1,0:T(8,128)S(1)} all-gather(f32[1,128,128]{2,1,0:T(8,128)S(1)} %copy-done.1), channel_id=1, replica_groups=mesh['row'=4,'col'=8] {'col'}, dimensions={0}, use_global_device_ids=true | all-gather | bytes 589824 | tf_op jit(solution)/shard_map/all_gather | solution.py:33
  71.6 0.6 copy-done.2
  72.3 27.2 %while.13 = (s32[]{:T(128)}, f32[1024,32]{0,1:T(8,128)S(1)}, s32[]{:T(128)}, s32[1,6]{1,0:T(1,128)S(1)}, f32[8,255,128]{2,1,0:T(8,128)S(1)}, /*index=5*/f32[8,12...) while((s32[]{:T(128)}, f32[1024,32]{0,1:T(8,128)S(1)}, ...), condition=%wide.region_1.0_spmd, body=%wide.region_0.0_spmd.sunk | while | flops 31367144 | bytes 556917 | solution.py:43
  72.9 0.6 constant_dynamic-slice_fusion.2
  75.9 0.3 convolution_subtract_fusion.2
  76.2 0.6 dynamic_update_slice.8
  77.5 0.6 constant_dynamic-slice_fusion.2
  80.5 0.3 convolution_subtract_fusion.2
  80.7 0.6 dynamic_update_slice.8
  82.0 0.6 constant_dynamic-slice_fusion.2
  85.0 0.3 convolution_subtract_fusion.2
  85.3 0.6 dynamic_update_slice.8
  86.5 0.6 constant_dynamic-slice_fusion.2
  89.8 0.6 dynamic_update_slice.8
  91.1 0.6 constant_dynamic-slice_fusion.2
  94.3 0.6 dynamic_update_slice.8
  95.6 0.6 constant_dynamic-slice_fusion.2
  98.6 0.3 convolution_subtract_fusion.2
  98.9 0.5 dynamic_update_slice.8
  99.5 7.4 %all_to_all.24 = f32[4,256,32]{1,2,0:T(8,128)S(1)} all-to-all(f32[4,256,32]{1,2,0:T(8,128)S(1)} %pad_maximum_fusion), channel_id=1, replica_groups=mesh['row'=4,'col'=8] {'row'}, dimensions={0} | all-to-all | bytes 262144 | tf_op jit(solution)/shard_map/all_to_all | solution.py:12
  106.9 0.8 copy.19
  (24 shorter events, 3.3 us)
Async XLA Ops:
  1.7 4.4 %copy-start = (f32[1,255,128]{2,0,1:T(1,128)S(1)}, f32[1,255,128]{2,0,1:T(1,128)}, u32[]{:S(2)}) copy-start(f32[1,255,128]{2,0,1:T(1,128)} %param.10) | copy-start | bytes 391684
  1.7 69.9 %all-to-all-start = ((f32[256,4,32]{0,2,1:T(8,128)}), f32[256,4,32]{0,2,1:T(8,128)S(1)}, u32[]{:S(2)}, u32[]{:S(2)}) async-start(f32[256,4,32]{0,2,1:T(8,128)} %bitcast.3), calls=%async_computation | async-start | bytes 262144 | tf_op jit(solution)/shard_map/all_to_all | solution.py:35
  6.0 34.2 %copy-start.1 = (f32[1,128,128]{2,1,0:T(8,128)S(1)}, f32[1,128,128]{2,1,0:T(8,128)}, u32[]{:S(2)}) copy-start(f32[1,128,128]{2,1,0:T(8,128)} %param.11) | copy-start | bytes 196612
  71.6 0.7 copy-start.2
